TPU v7x, 256 devices: a whole 4x4x8 slice. The times are simulated.
256 devices in a mesh: chan: 32 (over z, x_hi, core), row: 4 (over y), col: 2 (over x_lo).
Axes of the slice: x: 4 (x_hi: 2, x_lo: 2; x = x_hi * 2 + x_lo), y: 4, z: 8, core: 2. Of those that a mesh axis runs over, the one named last changes fastest.
Arguments:
- voltages: bfloat16 [1024, 262144], P('chan', ('row', 'col')), may hold values from -6 to 6
Outputs:
- visibilities: float32 [256, 2, 1024, 1024], P('chan', None, 'row', 'col')
All inputs are finite; a program needn't handle non-finite values.
Results may differ from a plain program's by a relative error of at most 0.0053.
Values may be sent and summed in bfloat16 or wider, within the bound.
No kernel may reach another device: no remote copies, remote signals or barrier semaphores. Data moves between devices by JAX's collectives and lax.ppermute only.
A program may use at most 128 MiB of HBM per device.

v0:
```python
import jax
import jax.numpy as jnp
from jax import lax
from jax.sharding import PartitionSpec as P

FFT_LEN = 512
TAPS = 8
CHANNELS = 256


def shifted(value, axis, by):
    length = lax.axis_size(axis)
    pairs = [(i, i + by) for i in range(length) if 0 <= i + by < length]
    return lax.ppermute(value, axis, pairs)


def window_table(taps, length):
    count = taps * length
    position = jnp.arange(count).astype(jnp.float32)
    offset = (position - count / 2 + 0.5) / length
    taper = 0.5 - 0.5 * jnp.cos(2.0 * jnp.pi * (position + 0.5) / count)
    values = jnp.sinc(offset) * taper
    values = values / jnp.sqrt(jnp.sum(values * values))
    return values.reshape(taps, length)


def fourier_table(channels, length):
    channel_index = jnp.arange(channels, dtype=jnp.int32)[:, None]
    sample_index = jnp.arange(length, dtype=jnp.int32)[None, :]
    phase = (channel_index * sample_index % length).astype(jnp.float32) * (2.0 * jnp.pi / length)
    return jnp.stack([jnp.cos(phase), -jnp.sin(phase)], axis=1).astype(jnp.bfloat16)


def per_device(voltages):
    local_inputs = voltages.shape[0]
    slot_spectra = voltages.shape[1] // FFT_LEN
    window = window_table(TAPS, FFT_LEN)
    table = fourier_table(CHANNELS, FFT_LEN)
    tail = voltages[:, (slot_spectra - TAPS + 1) * FFT_LEN :]
    earlier = shifted(tail, ("row", "col"), 1)
    extended = jnp.concatenate([earlier, voltages], axis=1).reshape(
        local_inputs, slot_spectra + TAPS - 1, FFT_LEN
    )
    total = jnp.zeros((local_inputs, slot_spectra, FFT_LEN), jnp.float32)
    for tap_index in range(TAPS):
        total = total + window[tap_index][None, None, :] * extended[
            :, tap_index : tap_index + slot_spectra, :
        ].astype(jnp.float32)
    filtered = total.astype(jnp.bfloat16)
    spectra = jnp.einsum(
        "kpn,isn->kpsi", table, filtered, preferred_element_type=jnp.float32
    ).astype(jnp.bfloat16)
    turned = lax.all_to_all(spectra, "chan", split_axis=0, concat_axis=3, tiled=True)
    inputs_all = turned.shape[3]
    row_count = lax.axis_size("row")
    col_count = lax.axis_size("col")
    row_block = inputs_all // row_count
    col_block = inputs_all // col_count
    spectra_total = slot_spectra * row_count * col_count
    row_start = lax.axis_index("row") * row_block
    col_start = lax.axis_index("col") * col_block
    piece = lax.all_gather(turned, ("row", "col"), axis=2, tiled=True)
    left = lax.dynamic_slice_in_dim(piece, row_start, row_block, 3)
    right = lax.dynamic_slice_in_dim(piece, col_start, col_block, 3)
    flipped = jnp.stack([left[:, 1], -left[:, 0]], axis=1)
    real_part = jnp.einsum("cpsi,cpsj->cij", left, right, preferred_element_type=jnp.float32)
    imag_part = jnp.einsum("cpsi,cpsj->cij", flipped, right, preferred_element_type=jnp.float32)
    summed = jnp.stack([real_part, imag_part], axis=1)
    return summed / spectra_total


def solution(mesh):
    placed = (P("chan", ("row", "col")),)
    return jax.shard_map(
        per_device,
        mesh=mesh,
        in_specs=placed,
        out_specs=P("chan", None, "row", "col"),
        check_vma=False,
    )
```

profile of v0, /device:TPU:1, one launch (start us, length us, event | category | flops | bytes accessed | tf_op | source)
XLA Modules:
  0.0 496.5 jit_solution(200310706514286712)
XLA Ops:
  6.5 0.0 all-gather.2.cloned.1.call-start
  6.5 1.0 slice.66
  7.5 4.0 collective-permute-start
  11.5 0.7 multiply_reduce_fusion
  12.2 2.2 negate_convert_fusion
  15.0 0.1 broadcast_divide_fusion
  15.1 0.6 collective-permute-done
  15.7 1.7 pad_maximum_fusion
  17.4 2.6 reshape.97
  20.1 11.7 %convert_bitcast_fusion = bf16[256,2,64,32]{0,2,1,3:T(8,128)(2,1)S(1)} fusion(bf16[32,71,512]{2,1,0:T(8,128)(2,1)} %reshape.97, f32[512]{0:T(512)S(1)} %get-tuple-element.8, f32[512]{0:T(512)S(1)} %get-tuple-element.9, f32[512]{0:T(512)S(1)} %get-tuple-element.10, f32[512]{0:T(512)S(1)} %get-tuple-element.11, f32[512]{0:T(512)S(1)} %get-tuple-element.12, ...), kind=kOutput, calls=%fused_computation.16 | convolution fusion | flops 1101004800 | bytes 19415040 | tf_op jit(solution)/shard_map/kpn,isn->kpsi/dot_general | solution.py:50
  31.8 7.6 %copy.12 = bf16[256,2,64,32]{2,1,3,0:T(2,128)(2,1)} copy(bf16[256,2,64,32]{0,2,1,3:T(8,128)(2,1)S(1)} %convert_bitcast_fusion) | data formatting | bytes 4194304 | tf_op jit(solution)/shard_map/convert_element_type | solution.py:52
  39.5 9.1 %reshape.102 = bf16[32,2,16384]{2,1,0:T(2,128)(2,1)S(1)} reshape(bf16[256,32,2,64]{3,2,1,0:T(2,128)(2,1)} %bitcast.26) | data formatting | bytes 4194304
  48.6 62.7 %all_to_all.18 = bf16[32,2,16384]{2,1,0:T(2,128)(2,1)} all-to-all(bf16[32,2,16384]{2,1,0:T(2,128)(2,1)S(1)} %reshape.102), channel_id=1, replica_groups=mesh['chan'=32,'row'=4,'col'=2] {'chan'}, dimensions={0} | all-to-all | bytes 4194304 | tf_op jit(solution)/shard_map/all_to_all | solution.py:53
  111.3 9.8 %reshape.103 = bf16[256,32,2,64]{3,2,1,0:T(2,128)(2,1)} reshape(bf16[32,2,16384]{2,1,0:T(2,128)(2,1)} %all_to_all.18) | data formatting | bytes 4194304
  121.1 3.2 copy.13
  124.3 2.9 copy.14
  127.2 4.8 copy.15
  132.0 0.0 all-gather.2.cloned.1.call-update
  132.0 327.7 %all-gather.2.cloned.1.call-done = bf16[8,2,512,1024]{3,2,1,0:T(8,128)(2,1)} async-done(((bf16[8,2,64,1024]{3,2,1,0:T(8,128)(2,1)}), bf16[8,2,512,1024]{3,2,1,0:T(8,128)(2,1)}) %all-gather.2.cloned.1.call-update) | async-done | bytes 16777232 | tf_op jit(solution)/shard_map/all_gather | solution.py:62
  459.7 4.1 constant_dynamic-slice_fusion
  463.8 0.0 copy-start
  463.8 9.4 %fusion.8 = f32[8,1,256,512]{3,2,0,1:T(8,128)} fusion(bf16[8,2,512,1024]{3,2,1,0:T(8,128)(2,1)} %all-gather.2.cloned.1.call-done, s32[]{:T(128)S(6)} %select_n.65, s32[]{:T(128)S(6)} %select_n.64), kind=kOutput, calls=%fused_computation.11 | convolution fusion | flops 2147483648 | bytes 16777224 | tf_op jit(solution)/shard_map/cpsi,cpsj->cij/dot_general | solution.py:66
  473.2 1.6 copy-done
  474.7 6.0 %fusion.13 = f32[8,1,256,512]{3,2,0,1:T(8,128)} fusion(bf16[8,2,512,1024]{3,2,1,0:T(8,128)(2,1)S(1)} %copy-done, s32[]{:T(128)S(6)} %select_n.65, bf16[8,1,512,256]{3,2,1,0:T(8,128)(2,1)} %get-tuple-element.6, bf16[8,1,512,256]{3,2,1,0:T(8,128)(2,1)S(1)} %get-tuple-element.5), kind=kOutput, calls=%fused_computation.12 | convolution fusion | flops 2149580800 | bytes 16777220 | tf_op jit(solution)/shard_map/cpsi,cpsj->cij/dot_general | solution.py:67
  480.7 4.5 maximum_multiply_fusion
  485.2 4.4 copy.18
  (1 shorter events, 0.0 us)
Async XLA Ops:
  6.5 453.2 %all-gather.2.cloned.1.call-start = ((), (), s32[]{:S(2)}) async-start(), calls=%async_computation.1 | async-start | bytes 18874368 | tf_op jit(solution)/shard_map/all_gather | solution.py:62
  7.5 8.2 %collective-permute-start = (bf16[32,3584]{1,0:T(8,128)(2,1)S(1)}, bf16[32,3584]{1,0:T(8,128)(2,1)S(1)}, u32[]{:S(2)}, u32[]{:S(2)}) collective-permute-start(bf16[32,3584]{1,0:T(8,128)(2,1)S(1)} %slice.66), channel_id=1, source_target_pairs={{0,1},{1,2},{2,3},{3,4},{4,5},{5,6},{6,7},{8,9},{9,10},{10,11},{11... | collective-permute-start | bytes 688136 | tf_op jit(solution)/shard_map/ppermute | solution.py:14
  463.8 10.9 %copy-start = (bf16[8,2,512,1024]{3,2,1,0:T(8,128)(2,1)S(1)}, bf16[8,2,512,1024]{3,2,1,0:T(8,128)(2,1)}, u32[]{:S(2)}) copy-start(bf16[8,2,512,1024]{3,2,1,0:T(8,128)(2,1)} %all-gather.2.cloned.1.call-done) | copy-start | bytes 50331652
Sparse Core Ops, SparseCore 0:
  132.1 327.5 all-gather.1
where the time goes:
time: 497 us
  waiting for transfers between devices  328 us (66%)
  blocking collectives  62.7 us (13%)
  local copies, waits for them, and re-layouts  47.1 us (9%)
  matrix products  27.1 us (5%)
  between operations  14.2 us (3%)
  other arithmetic  13.3 us (3%)
    all_gather x1, waiting for transfers between devices, per_device(): piece = lax.all_gather(turned, ('row', 'col'), axis=2, tiled=True)  328 us
    all_to_all x1, blocking collectives, per_device(): lax.all_to_all(spectra, 'chan', split_axis=0, concat_axis=3, tiled=True)  62.7 us
    unnamed x4, local copies, waits for them, and re-layouts  20.5 us
    dot_general x1, matrix products, per_device(): jnp.einsum('kpn,isn->kpsi', table, filtered, preferred_element_type=jnp.f...  11.7 us
    all_to_all x3, local copies, waits for them, and re-layouts, per_device(): lax.all_to_all(spectra, 'chan', split_axis=0, concat_axis=3, tiled=True)  10.9 us
  transfers between devices with their start and end apart: 2, of which 2 were waited for; matrix products, arithmetic and copies ran while one was open for 1% of the time, Pallas kernels for 0%

commit v1 on v0

--- a/solution.py
+++ b/solution.py
@@ -59,7 +59,10 @@
     spectra_total = slot_spectra * row_count * col_count
     row_start = lax.axis_index("row") * row_block
     col_start = lax.axis_index("col") * col_block
-    piece = lax.all_gather(turned, ("row", "col"), axis=2, tiled=True)
+    piece = jnp.concatenate(
+        lax.all_to_all(jnp.stack([turned] * lax.axis_size(("row", "col"))), ("row", "col"), 0, 0),
+        axis=2,
+    )
     left = lax.dynamic_slice_in_dim(piece, row_start, row_block, 3)
     right = lax.dynamic_slice_in_dim(piece, col_start, col_block, 3)
     flipped = jnp.stack([left[:, 1], -left[:, 0]], axis=1)

time: 497 us -> 352 us (0.71)
  waiting for transfers between devices: 328 us -> 184 us
  between operations: 14.2 us -> 0.78 us
  local copies, waits for them, and re-layouts: 47.1 us -> 58.4 us
  starting transfers between devices: 3.96 us -> 10.3 us
  matrix products: 27.1 us -> 21.9 us
    all_gather x1 -> x0, waiting for transfers between devices: 328 us -> none  [per_device(): piece = lax.all_gather(turned, ('row', 'col'), axis=2, tiled=True)]
    all_to_all x0 -> x1, waiting for transfers between devices: none -> 184 us  [per_device(): lax.all_to_all(jnp.stack([turned] * lax.axis_size(('row', 'col'))), ('row...]
    another operation x0 -> x2, local copies, waits for them, and re-layouts: none -> 9.52 us  [per_device(): jnp.stack([turned] * lax.axis_size(('row', 'col')))]
    reshape x0 -> x1, local copies, waits for them, and re-layouts: none -> 8.15 us  [per_device(): jnp.concatenate(lax.all_to_all(jnp.stack([turned] * lax.axis_size(('row',...]
    all_to_all x0 -> x1, starting transfers between devices: none -> 6.37 us  [per_device(): lax.all_to_all(jnp.stack([turned] * lax.axis_size(('row', 'col'))), ('row...]
    dot_general x1, matrix products: 9.38 us -> 4.33 us  [per_device(): jnp.einsum('cpsi,cpsj->cij', left, right, preferred_element_type=jnp.floa...]
    all_to_all x3 -> x2, local copies, waits for them, and re-layouts: 10.9 us -> 6.16 us  [per_device(): lax.all_to_all(spectra, 'chan', split_axis=0, concat_axis=3, tiled=True)]
    unnamed x4 -> x2, local copies, waits for them, and re-layouts: 20.5 us -> 18.9 us
where the time goes in v1:
time: 352 us; the launch traced here: 350 us
  waiting for transfers between devices  184 us (52%)
  blocking collectives  62.8 us (18%)
  local copies, waits for them, and re-layouts  58.4 us (17%)
  matrix products  21.9 us (6%)
  other arithmetic  11.4 us (3%)
  starting transfers between devices  10.3 us (3%)
    all_to_all x1, waiting for transfers between devices, per_device(): lax.all_to_all(jnp.stack([turned] * lax.axis_size(('row', 'col'))), ('row...  184 us
    all_to_all x1, blocking collectives, per_device(): lax.all_to_all(spectra, 'chan', split_axis=0, concat_axis=3, tiled=True)  62.8 us
    unnamed x2, local copies, waits for them, and re-layouts  18.9 us
    dot_general x1, matrix products, per_device(): jnp.einsum('kpn,isn->kpsi', table, filtered, preferred_element_type=jnp.f...  11.6 us
    another operation x2, local copies, waits for them, and re-layouts, per_device(): jnp.stack([turned] * lax.axis_size(('row', 'col')))  9.52 us
    reshape x1, local copies, waits for them, and re-layouts, per_device(): jnp.concatenate(lax.all_to_all(jnp.stack([turned] * lax.axis_size(('row',...  8.15 us
    convert_element_type x1, local copies, waits for them, and re-layouts, per_device(): spectra = jnp.einsum('kpn,isn->kpsi', table, filtered, preferred_element_...  7.64 us
  transfers between devices with their start and end apart: 2, of which 2 were waited for; matrix products, arithmetic and copies ran while one was open for 1% of the time, Pallas kernels for 0%

profile of v1, /device:TPU:1, one launch (start us, length us, event | category | flops | bytes accessed | tf_op | source)
XLA Modules:
  0.0 350.1 jit_solution(14333400283281498731)
XLA Ops:
  0.0 1.0 slice.66
  1.0 4.0 %collective-permute-start = (bf16[32,3584]{1,0:T(8,128)(2,1)S(1)}, bf16[32,3584]{1,0:T(8,128)(2,1)S(1)}, u32[]{:S(2)}, u32[]{:S(2)}) collective-permute-start(bf16[32,3584]{1,0:T(8,128)(2,1)S(1)} %slice.66), channel_id=1, source_target_pairs={{0,1},{1,2},{2,3},{3,4},{4,5},{5,6},{6,7},{8,9},{9,10},{10,11},{11... | collective-permute-start | bytes 688136 | tf_op jit(solution)/shard_map/ppermute | solution.py:14
  4.9 0.7 multiply_reduce_fusion
  5.6 2.2 negate_convert_fusion
  8.5 0.1 broadcast_divide_fusion
  8.6 0.6 collective-permute-done
  9.2 1.7 pad_maximum_fusion
  10.9 2.6 reshape.106
  13.6 11.6 %convert_bitcast_fusion = bf16[256,2,64,32]{0,2,1,3:T(8,128)(2,1)S(1)} fusion(bf16[32,71,512]{2,1,0:T(8,128)(2,1)} %reshape.106, f32[512]{0:T(512)S(1)} %get-tuple-element.8, f32[512]{0:T(512)S(1)} %get-tuple-element.9, f32[512]{0:T(512)S(1)} %get-tuple-element.10, f32[512]{0:T(512)S(1)} %get-tuple-element.11, f32[512]{0:T(512)S(1)} %get-tuple-element.12, ...), kind=kOutput, calls=%fused_computation.16 | convolution fusion | flops 1101004800 | bytes 19415040 | tf_op jit(solution)/shard_map/kpn,isn->kpsi/dot_general | solution.py:50
  25.2 7.6 %copy.11 = bf16[256,2,64,32]{2,1,3,0:T(2,128)(2,1)} copy(bf16[256,2,64,32]{0,2,1,3:T(8,128)(2,1)S(1)} %convert_bitcast_fusion) | data formatting | bytes 4194304 | tf_op jit(solution)/shard_map/convert_element_type | solution.py:52
  32.8 9.1 %reshape.113 = bf16[32,2,16384]{2,1,0:T(2,128)(2,1)S(1)} reshape(bf16[256,32,2,64]{3,2,1,0:T(2,128)(2,1)} %bitcast.31) | data formatting | bytes 4194304
  41.9 62.8 %all_to_all.20 = bf16[32,2,16384]{2,1,0:T(2,128)(2,1)} all-to-all(bf16[32,2,16384]{2,1,0:T(2,128)(2,1)S(1)} %reshape.113), channel_id=1, replica_groups=mesh['chan'=32,'row'=4,'col'=2] {'chan'}, dimensions={0} | all-to-all | bytes 4194304 | tf_op jit(solution)/shard_map/all_to_all | solution.py:53
  104.8 9.8 %reshape.114 = bf16[256,32,2,64]{3,2,1,0:T(2,128)(2,1)} reshape(bf16[32,2,16384]{2,1,0:T(2,128)(2,1)} %all_to_all.20) | data formatting | bytes 4194304
  114.5 3.2 copy.12
  117.8 2.9 copy.13
  120.7 3.5 %copy.14 = bf16[8,2,64,1024]{3,2,1,0:T(8,128)(2,1)S(1)} copy(bf16[8,2,64,1024]{2,3,1,0:T(8,128)(2,1)} %bitcast.34) | data formatting | bytes 4194304 | tf_op jit(solution)/shard_map/stack | solution.py:63
  124.3 6.0 %stack.34 = bf16[8,8,2,64,1024]{4,3,2,1,0:T(8,128)(2,1)} broadcast(bf16[8,2,64,1024]{3,2,1,0:T(8,128)(2,1)S(1)} %copy.14), dimensions={1,2,3,4} | broadcast | bytes 18874368 | tf_op jit(solution)/shard_map/stack | solution.py:63
  130.2 6.4 %all-to-all-start.1 = ((bf16[8,8,2,64,1024]{4,3,2,1,0:T(8,128)(2,1)}), bf16[8,8,2,64,1024]{4,3,2,1,0:T(8,128)(2,1)}, u32[]{:S(2)}, u32[]{:S(2)}) async-start(bf16[8,8,2,64,1024]{4,3,2,1,0:T(8,128)(2,1)} %stack.34), calls=%async_computation.1 | async-start | bytes 33554432 | tf_op jit(solution)/shard_map/all_to_all | solution.py:63
  136.6 183.8 %all-to-all-done.1 = bf16[8,8,2,64,1024]{4,3,2,1,0:T(8,128)(2,1)} async-done(((bf16[8,8,2,64,1024]{4,3,2,1,0:T(8,128)(2,1)}), bf16[8,8,2,64,1024]{4,3,2,1,0:T(8,128)(2,1)}, u32[]{:S(2)}, u32[]{:S(2)}) %all-to-all-start.1) | async-done | bytes 16777248 | tf_op jit(solution)/shard_map/all_to_all | solution.py:63
  320.4 8.1 %copy.15 = bf16[8,2,8,64,1024]{4,3,2,1,0:T(8,128)(2,1)S(1)} copy(bf16[8,2,8,64,1024]{4,3,1,0,2:T(8,128)(2,1)} %bitcast.7) | data formatting | bytes 33554432 | tf_op jit(solution)/shard_map/reshape | solution.py:62
  328.6 2.2 constant_dynamic-slice_fusion
  330.8 4.3 %fusion.8 = f32[8,1,256,512]{3,2,0,1:T(8,128)} fusion(bf16[8,2,512,1024]{3,2,1,0:T(8,128)(2,1)S(1)} %bitcast.29, s32[]{:T(128)S(6)} %select_n.65, s32[]{:T(128)S(6)} %select_n.64), kind=kOutput, calls=%fused_computation.11 | convolution fusion | flops 2147483648 | bytes 16777224 | tf_op jit(solution)/shard_map/cpsi,cpsj->cij/dot_general | solution.py:69
  335.1 6.0 %fusion.13 = f32[8,1,256,512]{3,2,0,1:T(8,128)} fusion(bf16[8,2,512,1024]{3,2,1,0:T(8,128)(2,1)S(1)} %bitcast.30, s32[]{:T(128)S(6)} %select_n.65, bf16[8,1,512,256]{3,2,1,0:T(8,128)(2,1)} %get-tuple-element.6, bf16[8,1,512,256]{3,2,1,0:T(8,128)(2,1)S(1)} %get-tuple-element.5), kind=kOutput, calls=%fused_computation.12 | convolution fusion | flops 2149580800 | bytes 16777220 | tf_op jit(solution)/shard_map/cpsi,cpsj->cij/dot_general | solution.py:70
  341.1 4.5 %maximum_multiply_fusion = f32[8,2,256,512]{3,2,0,1:T(8,128)S(1)} fusion(f32[8,1,256,512]{3,2,0,1:T(8,128)} %fusion.13, f32[8,1,256,512]{3,2,0,1:T(8,128)} %fusion.8), kind=kLoop, calls=%fused_computation | loop fusion | flops 4194304 | bytes 16777216 | tf_op jit(solution)/shard_map/div | solution.py:72
  345.7 4.4 %copy.18 = f32[8,2,256,512]{3,2,1,0:T(8,128)} copy(f32[8,2,256,512]{3,2,0,1:T(8,128)S(1)} %maximum_multiply_fusion) | data formatting | bytes 16777216 | tf_op jit(solution)/shard_map/div | solution.py:72
  (1 shorter events, 0.0 us)
Async XLA Ops:
  1.0 8.2 %collective-permute-start = (bf16[32,3584]{1,0:T(8,128)(2,1)S(1)}, bf16[32,3584]{1,0:T(8,128)(2,1)S(1)}, u32[]{:S(2)}, u32[]{:S(2)}) collective-permute-start(bf16[32,3584]{1,0:T(8,128)(2,1)S(1)} %slice.66), channel_id=1, source_target_pairs={{0,1},{1,2},{2,3},{3,4},{4,5},{5,6},{6,7},{8,9},{9,10},{10,11},{11... | collective-permute-start | bytes 688136 | tf_op jit(solution)/shard_map/ppermute | solution.py:14
  130.2 190.2 %all-to-all-start.1 = ((bf16[8,8,2,64,1024]{4,3,2,1,0:T(8,128)(2,1)}), bf16[8,8,2,64,1024]{4,3,2,1,0:T(8,128)(2,1)}, u32[]{:S(2)}, u32[]{:S(2)}) async-start(bf16[8,8,2,64,1024]{4,3,2,1,0:T(8,128)(2,1)} %stack.34), calls=%async_computation.1 | async-start | bytes 33554432 | tf_op jit(solution)/shard_map/all_to_all | solution.py:63
